TPU v7x, 256 devices: a whole 4x4x8 slice. The times are simulated.
256 devices in a mesh: feat: 16 (over z, y_hi), ex: 16 (over y_lo, x, core).
Axes of the slice: x: 4, y: 4 (y_hi: 2, y_lo: 2; y = y_hi * 2 + y_lo), z: 8, core: 2. Of those that a mesh axis runs over, the one named last changes fastest.
Arguments:
- activations: bfloat16 [1024, 28672], P('ex', 'feat'), may hold values from -6 to 6
- out_grads: bfloat16 [1024, 8192], P('feat', 'ex'), may hold values from -6 to 6
- basis_in: bfloat16 [28672, 28672], P('feat', 'ex'), may hold values from -0.03125 to 0.03125
- basis_out: bfloat16 [8192, 8192], P('ex', 'feat'), may hold values from -0.0625 to 0.0625
Outputs:
- correction: float32 [8192, 28672], P('feat', 'ex')
All inputs are finite; a program needn't handle non-finite values.
Results may differ from a plain program's by a relative error of at most 0.0034.
Values may be sent and summed in bfloat16 or wider, within the bound.
A program may use at most 64 MiB of HBM per device.

v0:
```python
import jax
import jax.numpy as jnp
from jax import lax
from jax.sharding import PartitionSpec as P

SEQ_LEN = 256


def per_device(activations, out_grads, basis_in, basis_out):
    partial_in = jnp.dot(
        lax.all_gather(activations, "ex", axis=0, tiled=True),
        basis_in,
        preferred_element_type=jnp.float32,
    )
    rotated_in = lax.psum(partial_in, "feat").astype(jnp.bfloat16)
    grad_all = lax.all_gather(out_grads, "feat", axis=0, tiled=True)
    out_share = lax.psum_scatter(
        jnp.dot(grad_all, basis_out, preferred_element_type=jnp.float32),
        "ex",
        scatter_dimension=0,
        tiled=True,
    )
    rotated_out = lax.all_gather(out_share.astype(jnp.bfloat16), "ex", axis=0, tiled=True)
    tokens_all = rotated_in.shape[0]
    seq_count = tokens_all // SEQ_LEN
    in_blocks = rotated_in.reshape(seq_count, SEQ_LEN, rotated_in.shape[1])
    out_blocks = rotated_out.reshape(seq_count, SEQ_LEN, rotated_out.shape[1])
    per_seq = jnp.einsum("nto,nti->noi", out_blocks, in_blocks, preferred_element_type=jnp.float32)
    total = jnp.sum(per_seq * per_seq, axis=0)
    return total / jnp.float32(tokens_all)


def solution(mesh):
    return jax.shard_map(
        per_device,
        mesh=mesh,
        in_specs=(P("ex", "feat"), P("feat", "ex"), P("feat", "ex"), P("ex", "feat")),
        out_specs=P("feat", "ex"),
        check_vma=False,
    )
```

profile of v0, /device:TPU:2, one launch (start us, length us, event | category | flops | bytes accessed | tf_op | source)
XLA Modules:
  0.0 540.3 jit_solution(13047750849756554427)
XLA Ops:
  6.5 0.0 copy-start
  6.5 0.0 all-gather.4.cloned.1.call-start
  6.5 0.7 all-gather.4.cloned.1.call-update
  7.3 0.0 reduce-scatter.2.cloned.1.call-start
  7.3 84.3 %all-gather.4.cloned.1.call-done = bf16[1024,512]{1,0:T(8,128)(2,1)} async-done(((bf16[64,512]{1,0:T(8,128)(2,1)}), bf16[1024,512]{1,0:T(8,128)(2,1)}) %all-gather.4.cloned.1.call-update) | async-done | bytes 1048592 | tf_op jit(solution)/shard_map/all_gather | solution.py:16
  91.7 0.0 copy-done
  91.7 3.2 fusion
  94.9 0.0 reduce-scatter.2.cloned.1.call-update
  94.9 0.0 all-gather.8.cloned.1.call-start
  95.0 0.7 all-gather.8.cloned.1.call-update
  95.7 0.0 all-gather.6.cloned.1.call-start
  95.7 58.4 %reduce-scatter.2.cloned.1.call-done = f32[64,512]{1,0:T(8,128)} async-done(((f32[1024,512]{1,0:T(8,128)}), f32[64,512]{1,0:T(8,128)}) %reduce-scatter.2.cloned.1.call-update) | async-done | bytes 131088 | tf_op jit(solution)/shard_map/reduce_scatter | solution.py:17
  154.1 1.5 convert_element_type.6
  155.7 0.0 all-gather.6.cloned.1.call-update
  155.7 41.8 %all-gather.8.cloned.1.call-done = bf16[1024,1792]{1,0:T(8,128)(2,1)} async-done(((bf16[64,1792]{1,0:T(8,128)(2,1)}), bf16[1024,1792]{1,0:T(8,128)(2,1)}) %all-gather.8.cloned.1.call-update) | async-done | bytes 3670032 | tf_op jit(solution)/shard_map/all_gather | solution.py:11
  197.4 12.2 %fusion.1 = f32[1024,1792]{1,0:T(8,128)} fusion(bf16[1024,1792]{1,0:T(8,128)(2,1)} %all-gather.8.cloned.1.call-done, bf16[1792,1792]{1,0:T(8,128)(2,1)} %param.6), kind=kOutput, calls=%fused_computation.3 | convolution fusion | flops 6576668672 | bytes 17432576 | tf_op jit(solution)/shard_map/dot_general | solution.py:10
  209.6 317.3 %all-reduce.1 = bf16[1024,1792]{1,0:T(8,128)(2,1)} all-reduce(f32[1024,1792]{1,0:T(8,128)} %fusion.1), channel_id=1, replica_groups=mesh['feat'=16,'ex'=16] {'feat'}, use_global_device_ids=true, to_apply=%region_1.0 | all-reduce | flops 1835008 | bytes 11010048 | tf_op jit(solution)/shard_map/psum | solution.py:15
  526.9 0.0 all-gather.6.cloned.1.call-done
  526.9 4.8 multiply_reduce_fusion
  531.7 2.1 broadcast_multiply_fusion
Async XLA Ops:
  6.5 85.1 %copy-start = (bf16[512,512]{1,0:T(8,128)(2,1)S(1)}, bf16[512,512]{1,0:T(8,128)(2,1)}, u32[]{:S(2)}) copy-start(bf16[512,512]{1,0:T(8,128)(2,1)} %param.7) | copy-start | bytes 1572868
  6.5 85.1 %all-gather.4.cloned.1.call-start = ((), (), s32[]{:S(2)}) async-start(), calls=%async_computation.1 | async-start | bytes 1114112 | tf_op jit(solution)/shard_map/all_gather | solution.py:16
  7.3 146.9 %reduce-scatter.2.cloned.1.call-start = ((), (), s32[]{:S(2)}) async-start(), calls=%async_computation.2 | async-start | bytes 2228224 | tf_op jit(solution)/shard_map/reduce_scatter | solution.py:17
  94.9 102.5 %all-gather.8.cloned.1.call-start = ((), (), s32[]{:S(2)}) async-start(), calls=%async_computation.4 | async-start | bytes 3899392 | tf_op jit(solution)/shard_map/all_gather | solution.py:11
  95.7 431.2 %all-gather.6.cloned.1.call-start = ((), (), s32[]{:S(2)}) async-start(), calls=%async_computation.3 | async-start | bytes 1114112 | tf_op jit(solution)/shard_map/all_gather | solution.py:23
Sparse Core Ops, SparseCore 0:
  9.9 81.6 all-gather.3
  95.0 59.0 reduce-scatter.1
  156.0 41.4 all-gather.7
  199.1 46.5 all-gather.5
where the time goes:
time: 540 us
  blocking collectives  317 us (59%)
  waiting for transfers between devices  186 us (34%)
  matrix products  20.2 us (4%)
  between operations  13.1 us (2%)
    psum x1, blocking collectives, per_device(): rotated_in = lax.psum(partial_in, 'feat').astype(jnp.bfloat16)  317 us
    all_gather x1, waiting for transfers between devices, per_device(): grad_all = lax.all_gather(out_grads, 'feat', axis=0, tiled=True)  84.3 us
    reduce_scatter x1, waiting for transfers between devices, per_device(): lax.psum_scatter(jnp.dot(grad_all, basis_out, preferred_element_type=jnp....  58.4 us
    all_gather x1, waiting for transfers between devices, per_device(): lax.all_gather(activations, 'ex', axis=0, tiled=True)  41.8 us
    dot_general x1, matrix products, per_device(): jnp.dot(lax.all_gather(activations, 'ex', axis=0, tiled=True), basis_in,...  12.2 us
  transfers between devices with their start and end apart: 4, of which 3 were waited for; matrix products, arithmetic and copies ran while one was open for 3% of the time, Pallas kernels for 0%

commit v1 on v0

--- a/solution.py
+++ b/solution.py
@@ -8,7 +8,9 @@
 
 def per_device(activations, out_grads, basis_in, basis_out):
     partial_in = jnp.dot(
-        lax.all_gather(activations, "ex", axis=0, tiled=True),
+        jnp.concatenate(
+            lax.all_to_all(jnp.stack([activations] * lax.axis_size("ex")), "ex", 0, 0), axis=0
+        ),
         basis_in,
         preferred_element_type=jnp.float32,
     )

time: 540 us -> 498 us (0.922)
  the two profiles are of different devices: /device:TPU:2 before, /device:TPU:30 now
where the time goes in v1:
time: 498 us
  blocking collectives  317 us (64%)
  waiting for transfers between devices  135 us (27%)
  matrix products  20.3 us (4%)
  between operations  13.1 us (3%)
  starting transfers between devices  5.78 us (1%)
    psum x1, blocking collectives, per_device(): rotated_in = lax.psum(partial_in, 'feat').astype(jnp.bfloat16)  317 us
    all_gather x1, waiting for transfers between devices, per_device(): grad_all = lax.all_gather(out_grads, 'feat', axis=0, tiled=True)  85.5 us
    reduce_scatter x1, waiting for transfers between devices, per_device(): lax.psum_scatter(jnp.dot(grad_all, basis_out, preferred_element_type=jnp....  48.5 us
    dot_general x1, matrix products, per_device(): jnp.dot(jnp.concatenate(lax.all_to_all(jnp.stack([activations] * lax.axis...  12.2 us
  transfers between devices with their start and end apart: 4, of which 2 were waited for; matrix products, arithmetic and copies ran while one was open for 4% of the time, Pallas kernels for 0%

profile of v1, /device:TPU:30, one launch (start us, length us, event | category | flops | bytes accessed | tf_op | source)
XLA Modules:
  0.0 497.7 jit_solution(15668292720832280003)
XLA Ops:
  6.5 0.0 copy-start
  6.5 0.0 all-gather.3.cloned.1.call-start
  6.5 0.7 all-gather.3.cloned.1.call-update
  7.3 3.1 stack.2
  10.4 5.7 %all-to-all-start = ((bf16[16,64,1792]{2,1,0:T(8,128)(2,1)}), bf16[16,64,1792]{2,1,0:T(8,128)(2,1)}, u32[]{:S(2)}, u32[]{:S(2)}) async-start(bf16[16,64,1792]{2,1,0:T(8,128)(2,1)} %stack.2), calls=%async_computation.1 | async-start | bytes 7340032 | tf_op jit(solution)/shard_map/all_to_all | solution.py:12
  16.1 0.0 reduce-scatter.2.cloned.1.call-start
  16.1 85.5 %all-gather.3.cloned.1.call-done = bf16[1024,512]{1,0:T(8,128)(2,1)} async-done(((bf16[64,512]{1,0:T(8,128)(2,1)}), bf16[1024,512]{1,0:T(8,128)(2,1)}) %all-gather.3.cloned.1.call-update) | async-done | bytes 1048592 | tf_op jit(solution)/shard_map/all_gather | solution.py:18
  101.6 0.0 copy-done
  101.6 3.3 fusion
  104.9 0.0 reduce-scatter.2.cloned.1.call-update
  104.9 0.0 all-gather.5.cloned.1.call-start
  105.0 0.0 all-to-all-done
  105.0 12.2 %fusion.1 = f32[1024,1792]{1,0:T(8,128)} fusion(bf16[1024,1792]{1,0:T(8,128)(2,1)} %bitcast.1, bf16[1792,1792]{1,0:T(8,128)(2,1)} %param.6), kind=kOutput, calls=%fused_computation.3 | convolution fusion | flops 6576668672 | bytes 17432576 | tf_op jit(solution)/shard_map/dot_general | solution.py:10
  117.2 48.5 %reduce-scatter.2.cloned.1.call-done = f32[64,512]{1,0:T(8,128)} async-done(((f32[1024,512]{1,0:T(8,128)}), f32[64,512]{1,0:T(8,128)}) %reduce-scatter.2.cloned.1.call-update) | async-done | bytes 131088 | tf_op jit(solution)/shard_map/reduce_scatter | solution.py:19
  165.7 1.5 convert_element_type.6
  167.2 0.0 all-gather.5.cloned.1.call-update
  167.2 317.1 %all-reduce.1 = bf16[1024,1792]{1,0:T(8,128)(2,1)} all-reduce(f32[1024,1792]{1,0:T(8,128)} %fusion.1), channel_id=1, replica_groups=mesh['feat'=16,'ex'=16] {'feat'}, use_global_device_ids=true, to_apply=%region_1.0 | all-reduce | flops 1835008 | bytes 11010048 | tf_op jit(solution)/shard_map/psum | solution.py:17
  484.4 0.0 all-gather.5.cloned.1.call-done
  484.4 4.8 multiply_reduce_fusion
  489.1 2.1 broadcast_multiply_fusion
Async XLA Ops:
  6.5 95.1 %copy-start = (bf16[512,512]{1,0:T(8,128)(2,1)S(1)}, bf16[512,512]{1,0:T(8,128)(2,1)}, u32[]{:S(2)}) copy-start(bf16[512,512]{1,0:T(8,128)(2,1)} %param.7) | copy-start | bytes 1572868
  6.5 95.1 %all-gather.3.cloned.1.call-start = ((), (), s32[]{:S(2)}) async-start(), calls=%async_computation.2 | async-start | bytes 1114112 | tf_op jit(solution)/shard_map/all_gather | solution.py:18
  10.4 94.6 %all-to-all-start = ((bf16[16,64,1792]{2,1,0:T(8,128)(2,1)}), bf16[16,64,1792]{2,1,0:T(8,128)(2,1)}, u32[]{:S(2)}, u32[]{:S(2)}) async-start(bf16[16,64,1792]{2,1,0:T(8,128)(2,1)} %stack.2), calls=%async_computation.1 | async-start | bytes 7340032 | tf_op jit(solution)/shard_map/all_to_all | solution.py:12
  16.1 149.6 %reduce-scatter.2.cloned.1.call-start = ((), (), s32[]{:S(2)}) async-start(), calls=%async_computation.3 | async-start | bytes 2228224 | tf_op jit(solution)/shard_map/reduce_scatter | solution.py:19
  104.9 379.4 %all-gather.5.cloned.1.call-start = ((), (), s32[]{:S(2)}) async-start(), calls=%async_computation.4 | async-start | bytes 1114112 | tf_op jit(solution)/shard_map/all_gather | solution.py:25
Sparse Core Ops, SparseCore 0:
  9.9 91.6 all-gather.2
  105.0 60.5 reduce-scatter.1
  167.5 43.4 all-gather.4
